TPU v7x, 256 devices: a whole 4x4x8 slice. The times are simulated.
256 devices in a mesh: sub: 64 (over z, y, core), rhs: 4 (over x).
Axes of the slice: x: 4, y: 4, z: 8, core: 2. Of those that a mesh axis runs over, the one named last changes fastest.
Arguments:
- stiffness: float32 [3072, 4, 9216], P('sub'), may hold values from -1 to 2, as said below
- precond: float32 [3072, 9216], P('sub'), may hold values from -0.625 to 0.625
- rhs_vec: float32 [8, 294912], P('rhs', 'sub'), may hold values from -50 to 50
- cotangent: float32 [8, 294912], P('rhs', 'sub'), may hold values from -6 to 6
- col_index: int32 [3072, 4], P('sub'), may hold values from 0 to 59, as said below
- send_rows: int32 [64, 12], P('sub'), may hold values from 0 to 47, as said below
- counts: int32 [64], P('sub'), may hold values from 12 to 48, as said below
Outputs:
- solution: float32 [8, 294912], P('rhs', 'sub')
- grad_precond: float32 [3072, 9216], P('sub')
Inputs may be any that keep to these rules, and one draw needn't show every extreme that they name: `counts`: at least one subdomain has 48 live block rows. `send_rows`: for subdomain s, entries 0 to 5 are distinct live rows below counts[s] // 2 in increasing order, the first of them 0; entries 6 to 11 are distinct live rows from counts[s] // 2 on in increasing order, the last of them counts[s] - 1. Interface row j of the first group of subdomain s is coupled with interface row j of the second group of subdomain s - 1. `col_index`: index 6 + n is block n of the subdomain; indices below 6 and from 54 on are the blocks received from the previous and the next subdomain. Slot 0 of row n is 6 + n. A slot other than slot 0 that names 6 + n holds a zero block; rows that are not live hold only slot 0's block. `stiffness`: the operator A is symmetric and positive definite.
All inputs are finite; a program needn't handle non-finite values.
Results may differ from a plain program's by a relative error of at most 0.0003.
Values sent between devices are 32-bit elements; how exact they have to be, the bound alone decides.
A program may use at most 128 MiB of HBM per device.

v0:
```python
import jax
import jax.numpy as jnp
from jax import lax
from jax.sharding import PartitionSpec as P

BS = 96
K = 4
NBLK = 48
IF = 6
ITERS = 4
highest = lax.Precision.HIGHEST


def with_halo(array, sides, width):
    for axis, dim in sides:
        size, length = (lax.axis_size(axis), array.shape[dim])
        up = [(i, (i + 1) % size) for i in range(size - 1)]
        down = [(j, i) for i, j in up]
        last = lax.slice_in_dim(array, length - width, length, axis=dim)
        initial = lax.slice_in_dim(array, 0, width, axis=dim)
        before = lax.ppermute(last, axis, up)
        after = lax.ppermute(initial, axis, down)
        array = jnp.concatenate([before, array, after], axis=dim)
    return array


def local_dot(first_vec, second_vec):
    return jnp.sum(first_vec * second_vec, axis=(1, 2))


def widen(scalars):
    return scalars[:, None, None]


def precond_apply(weights, vector):
    projected = jnp.einsum("nab,rnb->rna", weights, vector, precision=highest)
    return (projected, vector + jnp.einsum("nab,rna->rnb", weights, projected, precision=highest))


def block_product(blocks, gathered):
    return jnp.einsum("nkab,rnkb->rna", blocks, gathered, precision=highest)


def stiff_apply(vector, blocks, columns, sending):
    outgoing = jnp.take(vector, sending, axis=1)
    framed = with_halo(outgoing, (("sub", 1),), IF)
    extended = jnp.concatenate([framed[:, :IF], vector, framed[:, 3 * IF :]], axis=1)
    return block_product(blocks, jnp.take(extended, columns, axis=1))


def norm_sum(first_vec, second_vec):
    return lax.psum(local_dot(first_vec, second_vec), "sub")


def grad_term(projected, zeta_bar, weight_zeta, resid_vec):
    first_part = jnp.einsum("rna,rnb->nab", projected, zeta_bar, precision=highest)
    return first_part + jnp.einsum("rna,rnb->nab", weight_zeta, resid_vec, precision=highest)


def shards(stiffness, precond, rhs_vec, cotangent, col_index, send_rows, counts):
    rhs_all, cot_all = (rhs_vec, cotangent)
    local_rhs = rhs_all.shape[0]
    blocks = stiffness.reshape(NBLK, K, BS, BS)
    weights = precond.reshape(NBLK, BS, BS)
    live_count = counts[0]
    sending = send_rows[0]
    live_mask = (jnp.arange(NBLK) < live_count).astype(jnp.float32)
    source = rhs_all.reshape(local_rhs, NBLK, BS) * live_mask[None, :, None]
    target = cot_all.reshape(local_rhs, NBLK, BS)
    residual = source
    first_proj, precon = precond_apply(weights, residual)
    first_res = residual
    direction = precon
    norm_now = norm_sum(residual, precon)
    solution = jnp.zeros_like(source)
    history = []
    for iteration in range(ITERS):
        applied = stiff_apply(direction, blocks, col_index, sending)
        curvature = lax.psum(local_dot(direction, applied), "sub")
        step_len = norm_now / curvature
        solution = solution + widen(step_len) * direction
        residual = residual - widen(step_len) * applied
        record = [direction, applied, step_len, curvature, norm_now]
        if iteration + 1 < ITERS:
            projected, precon = precond_apply(weights, residual)
            norm_next = norm_sum(residual, precon)
            ratio = norm_next / norm_now
            record = record + [residual, precon, projected, norm_next, ratio]
            direction = precon + widen(ratio) * direction
            norm_now = norm_next
        history.append(record)
    dir_bar = jnp.zeros_like(source)
    res_bar = jnp.zeros_like(source)
    norm_bar = jnp.zeros((local_rhs,), jnp.float32)
    grad_sum = jnp.zeros((NBLK, BS, BS), jnp.float32)
    for iteration in reversed(range(ITERS)):
        direction, applied, step_len, curvature, norm_now = history[iteration][:5]
        if iteration + 1 < ITERS:
            resid_next, precon, projected, norm_next, ratio = history[iteration][5:]
            ratio_bar, cot_dir = lax.psum(
                (local_dot(dir_bar, direction), local_dot(target, direction)), "sub"
            )
            norm_full = norm_bar + ratio_bar / norm_now
            zeta_bar = dir_bar + widen(norm_full) * resid_next
            weight_zeta, mapped = precond_apply(weights, zeta_bar)
            res_bar = res_bar + widen(norm_full) * precon + mapped
            res_image = lax.psum(local_dot(res_bar, applied), "sub")
            grad_sum = grad_sum + grad_term(projected, zeta_bar, weight_zeta, resid_next)
            dir_new = widen(ratio) * dir_bar
            norm_new = -ratio_bar * norm_next / (norm_now * norm_now)
        else:
            cot_dir = lax.psum(local_dot(target, direction), "sub")
            res_image = jnp.zeros_like(cot_dir)
            dir_new = jnp.zeros_like(source)
            norm_new = jnp.zeros_like(cot_dir)
        step_bar = cot_dir - res_image
        curv_bar = -step_bar * step_len / curvature
        dir_new = dir_new + widen(step_len) * target + widen(curv_bar) * applied
        image_bar = widen(curv_bar) * direction - widen(step_len) * res_bar
        dir_bar = dir_new + stiff_apply(image_bar, blocks, col_index, sending)
        norm_bar = norm_new + step_bar / curvature
    zeta_bar = dir_bar + widen(norm_bar) * first_res
    weight_zeta = jnp.einsum("nab,rnb->rna", weights, zeta_bar, precision=highest)
    grad_sum = grad_sum + grad_term(first_proj, zeta_bar, weight_zeta, first_res)
    grad_sum = lax.psum(grad_sum, "rhs")
    flat_solution = solution.reshape(local_rhs, NBLK * BS)
    return (flat_solution, grad_sum.reshape(NBLK, BS * BS))


def solution(mesh):
    in_specs = (
        P("sub", None, None),
        P("sub", None),
        P("rhs", "sub"),
        P("rhs", "sub"),
        P("sub", None),
        P("sub", None),
        P("sub"),
    )
    out_specs = (P("rhs", "sub"), P("sub", None))
    return jax.shard_map(shards, mesh=mesh, in_specs=in_specs, out_specs=out_specs, check_vma=False)
```

profile of v0, /device:TPU:1, one launch (start us, length us, event | category | flops | bytes accessed | tf_op | source)
XLA Modules:
  0.0 1994.4 jit_solution(11728397006781931206)
XLA Ops:
  10.1 2.2 reshape.53
  12.3 3.8 convolution_bitcast_fusion.22
  16.1 2.1 fusion.14
  18.9 4.6 collective-permute-start
  23.5 1.9 collective-permute-start.1
  25.8 10.6 reshape.54
  37.3 10.5 multiply_reduce_fusion.16
  47.8 127.8 %all-reduce.4 = (f32[2]{0:T(128)S(1)}, f32[2]{0:T(128)S(1)}) all-reduce(f32[2]{0:T(128)S(1)} %get-tuple-element.10, f32[2]{0:T(128)S(1)} %get-tuple-element.9), channel_id=1, replica_groups=mesh['sub'=64,'rhs'=4] {'sub'}, use_global_device_ids=true, to_apply=%region_1.0 | all-reduce | flops 4 | bytes 32 | tf_op jit(solution)/shard_map/psum | solution.py:52
  175.8 3.8 convolution_bitcast_fusion.20
  179.5 2.2 multiply_reduce_fusion.15
  181.7 127.4 %psum.135 = f32[2]{0:T(128)S(1)} all-reduce(f32[2]{0:T(128)S(1)} %get-tuple-element.44), channel_id=1, replica_groups=mesh['sub'=64,'rhs'=4] {'sub'}, use_global_device_ids=true, to_apply=%region_5.8 | all-reduce | flops 2 | bytes 16 | tf_op jit(solution)/shard_map/psum | solution.py:52
  309.9 1.9 collective-permute-start.2
  311.8 2.4 collective-permute-start.3
  314.3 2.5 collective-permute-done.3
  317.7 10.5 multiply_reduce_fusion.14
  328.2 122.2 %psum.136 = f32[2]{0:T(128)S(1)} all-reduce(f32[2]{0:T(128)S(1)} %get-tuple-element.46), channel_id=1, replica_groups=mesh['sub'=64,'rhs'=4] {'sub'}, use_global_device_ids=true, to_apply=%region_7.10 | all-reduce | flops 2 | bytes 16 | tf_op jit(solution)/shard_map/psum | solution.py:79
  450.5 3.8 convolution_bitcast_fusion.18
  454.2 2.2 multiply_reduce_fusion.13
  456.5 125.9 %psum.137 = f32[2]{0:T(128)S(1)} all-reduce(f32[2]{0:T(128)S(1)} %get-tuple-element.48), channel_id=1, replica_groups=mesh['sub'=64,'rhs'=4] {'sub'}, use_global_device_ids=true, to_apply=%region_9.12 | all-reduce | flops 2 | bytes 16 | tf_op jit(solution)/shard_map/psum | solution.py:52
  585.1 2.4 collective-permute-start.5
  587.5 2.5 collective-permute-done.5
  591.0 10.5 multiply_reduce_fusion.12
  601.5 122.2 %psum.138 = f32[2]{0:T(128)S(1)} all-reduce(f32[2]{0:T(128)S(1)} %get-tuple-element.50), channel_id=1, replica_groups=mesh['sub'=64,'rhs'=4] {'sub'}, use_global_device_ids=true, to_apply=%region_11.14 | all-reduce | flops 2 | bytes 16 | tf_op jit(solution)/shard_map/psum | solution.py:79
  723.8 3.8 convolution_bitcast_fusion.16
  727.6 2.2 multiply_reduce_fusion.11
  729.8 125.9 %psum.139 = f32[2]{0:T(128)S(1)} all-reduce(f32[2]{0:T(128)S(1)} %get-tuple-element.52), channel_id=1, replica_groups=mesh['sub'=64,'rhs'=4] {'sub'}, use_global_device_ids=true, to_apply=%region_13.16 | all-reduce | flops 2 | bytes 16 | tf_op jit(solution)/shard_map/psum | solution.py:52
  858.5 2.4 collective-permute-start.7
  861.0 2.4 collective-permute-done.7
  864.3 11.1 multiply_reduce_fusion.1
  875.5 122.0 %all-reduce.3 = (f32[2]{0:T(128)S(1)}, f32[2]{0:T(128)S(1)}) all-reduce(f32[2]{0:T(128)S(1)} %get-tuple-element.6, f32[2]{0:T(128)S(1)} %get-tuple-element.5), channel_id=1, replica_groups=mesh['sub'=64,'rhs'=4] {'sub'}, use_global_device_ids=true, to_apply=%region_15.18 | all-reduce | flops 4 | bytes 32 | tf_op jit(solution)/shard_map/psum | solution.py:79
  1000.7 4.2 collective-permute-start.9
  1006.6 10.5 multiply_reduce_fusion.8
  1017.1 123.4 %psum.142 = f32[2]{0:T(128)S(1)} all-reduce(f32[2]{0:T(128)S(1)} %get-tuple-element.55), channel_id=1, replica_groups=mesh['sub'=64,'rhs'=4] {'sub'}, use_global_device_ids=true, to_apply=%region_19.22 | all-reduce | flops 2 | bytes 16 | tf_op jit(solution)/shard_map/psum | solution.py:100
  1140.6 3.8 convolution_bitcast_fusion.14
  1144.4 2.2 multiply_reduce_fusion.6
  1146.6 5.2 fusion.64
  1151.9 124.5 %all-reduce.2 = (f32[2]{0:T(128)S(1)}, f32[2]{0:T(128)S(1)}) all-reduce(f32[2]{0:T(128)S(1)} %copy-done.43, f32[2]{0:T(128)S(1)} %get-tuple-element.57), channel_id=1, replica_groups=mesh['sub'=64,'rhs'=4] {'sub'}, use_global_device_ids=true, to_apply=%region_21.24 | all-reduce | flops 4 | bytes 32 | tf_op jit(solution)/shard_map/psum | solution.py:100
  1279.7 2.6 collective-permute-start.11
  1282.2 5.4 fusion.63
  1288.6 10.5 multiply_reduce_fusion.5
  1299.1 123.0 %psum.145 = f32[2]{0:T(128)S(1)} all-reduce(f32[2]{0:T(128)S(1)} %get-tuple-element.59), channel_id=1, replica_groups=mesh['sub'=64,'rhs'=4] {'sub'}, use_global_device_ids=true, to_apply=%region_25.28 | all-reduce | flops 2 | bytes 16 | tf_op jit(solution)/shard_map/psum | solution.py:100
  1422.2 3.8 convolution_bitcast_fusion.12
  1426.0 2.2 multiply_reduce_fusion.3
  1428.2 5.2 fusion.66
  1433.5 125.2 %all-reduce.1 = (f32[2]{0:T(128)S(1)}, f32[2]{0:T(128)S(1)}) all-reduce(f32[2]{0:T(128)S(1)} %copy-done.42, f32[2]{0:T(128)S(1)} %get-tuple-element.61), channel_id=1, replica_groups=mesh['sub'=64,'rhs'=4] {'sub'}, use_global_device_ids=true, to_apply=%region_27.30 | all-reduce | flops 4 | bytes 32 | tf_op jit(solution)/shard_map/psum | solution.py:100
  1559.4 1.9 collective-permute-start.12
  1561.3 2.7 collective-permute-start.13
  1564.0 5.3 fusion.65
  1570.2 10.5 multiply_reduce_fusion.2
  1580.7 123.3 %psum.148 = f32[2]{0:T(128)S(1)} all-reduce(f32[2]{0:T(128)S(1)} %get-tuple-element.63), channel_id=1, replica_groups=mesh['sub'=64,'rhs'=4] {'sub'}, use_global_device_ids=true, to_apply=%region_31.34 | all-reduce | flops 2 | bytes 16 | tf_op jit(solution)/shard_map/psum | solution.py:100
  1704.1 3.8 convolution_bitcast_fusion.10
  1707.9 2.2 multiply_reduce_fusion
  1710.1 5.2 fusion.68
  1715.4 125.2 %all-reduce = (f32[2]{0:T(128)S(1)}, f32[2]{0:T(128)S(1)}) all-reduce(f32[2]{0:T(128)S(1)} %copy-done.41, f32[2]{0:T(128)S(1)} %get-tuple-element.65), channel_id=1, replica_groups=mesh['sub'=64,'rhs'=4] {'sub'}, use_global_device_ids=true, to_apply=%region_33.36 | all-reduce | flops 4 | bytes 32 | tf_op jit(solution)/shard_map/psum | solution.py:100
  1841.3 1.9 collective-permute-start.14
  1843.3 2.6 collective-permute-start.15
  1845.9 5.3 fusion.67
  1852.1 10.8 fusion.1
  1862.9 3.8 convolution_bitcast_fusion.8
  1866.7 3.9 fusion.69
  1870.6 4.3 add_add_fusion
  1874.9 2.5 reshape.57
  1878.2 106.4 %all-reduce.7.cloned.1.call-done = f32[48,9216]{1,0:T(8,128)} async-done(((f32[48,9216]{1,0:T(8,128)}), f32[48,9216]{1,0:T(8,128)}) %all-reduce.7.cloned.1.call-update) | async-done | bytes 1769488 | tf_op jit(solution)/shard_map/psum | solution.py:125
  1984.6 2.8 copy.72
  (192 shorter events, 26.9 us)
Async XLA Ops:
  7.2 1977.4 %all-reduce.7.cloned.1.call-start = ((), (), s32[]{:S(2)}) async-start(), calls=%async_computation | async-start | bytes 3538944 | tf_op jit(solution)/shard_map/psum | solution.py:125
  12.3 13.1 copy-start.13
  18.9 17.5 collective-permute-start
  23.5 12.9 collective-permute-start.1
  175.6 6.1 copy-start.44
  175.6 133.5 %copy-start.19 = (f32[2]{0:T(128)}, f32[2]{0:T(128)S(1)}, u32[]{:S(2)}) copy-start(f32[2]{0:T(128)S(1)} %get-tuple-element.19) | copy-start | bytes 28
  179.5 148.7 %copy-start.6 = (f32[2,48,96]{2,0,1:T(2,128)}, f32[2,48,96]{2,0,1:T(2,128)S(1)}, u32[]{:S(2)}) copy-start(f32[2,48,96]{2,0,1:T(2,128)S(1)} %convolution_bitcast_fusion.20) | copy-start | bytes 110596
  309.1 0.7 copy-start.14
  309.9 4.3 collective-permute-start.2
  311.8 4.9 collective-permute-start.3
  450.4 6.1 copy-start.21
  454.2 128.2 %copy-start.8 = (f32[2,48,96]{2,0,1:T(2,128)}, f32[2,48,96]{2,0,1:T(2,128)S(1)}, u32[]{:S(2)}) copy-start(f32[2,48,96]{2,0,1:T(2,128)S(1)} %convolution_bitcast_fusion.18) | copy-start | bytes 110596
  582.4 19.0 copy-start.16
  583.2 4.3 collective-permute-start.4
  585.1 4.9 collective-permute-start.5
  723.7 6.1 copy-start.24
  723.8 137.1 %copy-start.12 = (f32[2,4608]{1,0:T(2,128)S(1)}, f32[2,4608]{1,0:T(2,128)}, u32[]{:S(2)}) copy-start(f32[2,4608]{1,0:T(2,128)} %param.14) | copy-start | bytes 110596
  727.6 130.9 %copy-start.10 = (f32[2,48,96]{2,0,1:T(2,128)}, f32[2,48,96]{2,0,1:T(2,128)S(1)}, u32[]{:S(2)}) copy-start(f32[2,48,96]{2,0,1:T(2,128)S(1)} %convolution_bitcast_fusion.16) | copy-start | bytes 110596
  855.8 141.7 %copy-start.27 = (f32[2]{0:T(128)}, f32[2]{0:T(128)S(1)}, u32[]{:S(2)}) copy-start(f32[2]{0:T(128)S(1)} %psum.139) | copy-start | bytes 28
  855.8 19.7 copy-start.18
  856.5 4.5 collective-permute-start.6
  858.5 4.9 collective-permute-start.7
  997.4 0.6 copy-start.37
  997.5 0.6 copy-start.39
  998.8 6.2 collective-permute-start.8
  1000.7 4.9 collective-permute-start.9
  1006.6 134.0 %copy-start.38 = (f32[2]{0:T(128)S(1)}, f32[2]{0:T(128)}, u32[]{:S(2)}) copy-start(f32[2]{0:T(128)} %copy-done.37) | copy-start | bytes 28
  1006.6 133.9 %copy-start.40 = (f32[2]{0:T(128)S(1)}, f32[2]{0:T(128)}, u32[]{:S(2)}) copy-start(f32[2]{0:T(128)} %copy-done.39) | copy-start | bytes 28
  1140.5 6.1 copy-start.31
  1144.4 7.5 copy-start.43
  1144.4 132.0 %copy-start.25 = (f32[2]{0:T(128)S(1)}, f32[2]{0:T(128)}, u32[]{:S(2)}) copy-start(f32[2]{0:T(128)} %copy-done.24) | copy-start | bytes 28
  1144.4 137.8 %copy-start.11 = (f32[2,48,96]{2,0,1:T(2,128)S(1)}, f32[2,48,96]{2,0,1:T(2,128)}, u32[]{:S(2)}) copy-start(f32[2,48,96]{2,0,1:T(2,128)} %copy-done.10) | copy-start | bytes 110596
  1276.4 0.5 copy-start.33
  1276.4 0.6 copy-start.35
  1277.7 9.9 collective-permute-start.10
  1279.7 8.0 collective-permute-start.11
  1288.5 133.6 %copy-start.26 = (f32[2]{0:T(128)S(1)}, f32[2]{0:T(128)}, u32[]{:S(2)}) copy-start(f32[2]{0:T(128)} %copy-done.24) | copy-start | bytes 28
  1288.5 133.6 %copy-start.28 = (f32[2]{0:T(128)S(1)}, f32[2]{0:T(128)}, u32[]{:S(2)}) copy-start(f32[2]{0:T(128)} %copy-done.27) | copy-start | bytes 28
  1288.5 133.5 %copy-start.32 = (f32[2]{0:T(128)S(1)}, f32[2]{0:T(128)}, u32[]{:S(2)}) copy-start(f32[2]{0:T(128)} %copy-done.31) | copy-start | bytes 28
  1288.5 133.5 %copy-start.34 = (f32[2]{0:T(128)S(1)}, f32[2]{0:T(128)}, u32[]{:S(2)}) copy-start(f32[2]{0:T(128)} %copy-done.33) | copy-start | bytes 28
  1288.5 133.5 %copy-start.36 = (f32[2]{0:T(128)S(1)}, f32[2]{0:T(128)}, u32[]{:S(2)}) copy-start(f32[2]{0:T(128)} %copy-done.35) | copy-start | bytes 28
  1422.1 3.9 copy-start.29
  1426.0 7.5 copy-start.42
  1426.0 132.6 %copy-start.22 = (f32[2]{0:T(128)S(1)}, f32[2]{0:T(128)}, u32[]{:S(2)}) copy-start(f32[2]{0:T(128)} %copy-done.21) | copy-start | bytes 28
  1426.0 138.0 %copy-start.9 = (f32[2,48,96]{2,0,1:T(2,128)S(1)}, f32[2,48,96]{2,0,1:T(2,128)}, u32[]{:S(2)}) copy-start(f32[2,48,96]{2,0,1:T(2,128)} %copy-done.8) | copy-start | bytes 110596
  1428.2 142.0 %copy-start.17 = (f32[2]{0:T(128)S(1)}, f32[2]{0:T(128)}, u32[]{:S(2)}) copy-start(f32[2]{0:T(128)} %copy-done.16) | copy-start | bytes 28
  1559.4 9.9 collective-permute-start.12
  1561.3 8.0 collective-permute-start.13
  1570.2 133.8 %copy-start.20 = (f32[2]{0:T(128)S(1)}, f32[2]{0:T(128)}, u32[]{:S(2)}) copy-start(f32[2]{0:T(128)} %copy-done.19) | copy-start | bytes 28
  1570.2 133.8 %copy-start.23 = (f32[2]{0:T(128)S(1)}, f32[2]{0:T(128)}, u32[]{:S(2)}) copy-start(f32[2]{0:T(128)} %copy-done.21) | copy-start | bytes 28
  1570.2 133.8 %copy-start.30 = (f32[2]{0:T(128)S(1)}, f32[2]{0:T(128)}, u32[]{:S(2)}) copy-start(f32[2]{0:T(128)} %copy-done.29) | copy-start | bytes 28
  1707.9 7.5 copy-start.41
  1707.9 132.6 %copy-start.45 = (f32[2]{0:T(128)S(1)}, f32[2]{0:T(128)}, u32[]{:S(2)}) copy-start(f32[2]{0:T(128)} %copy-done.44) | copy-start | bytes 28
  1707.9 138.0 %copy-start.7 = (f32[2,48,96]{2,0,1:T(2,128)S(1)}, f32[2,48,96]{2,0,1:T(2,128)}, u32[]{:S(2)}) copy-start(f32[2,48,96]{2,0,1:T(2,128)} %copy-done.6) | copy-start | bytes 110596
  1710.1 142.0 %copy-start.15 = (f32[2]{0:T(128)S(1)}, f32[2]{0:T(128)}, u32[]{:S(2)}) copy-start(f32[2]{0:T(128)} %copy-done.14) | copy-start | bytes 28
  1841.3 9.8 collective-permute-start.14
  1843.3 7.9 collective-permute-start.15
  1852.1 18.4 copy-start.2
  1852.1 18.4 copy-start.3
  1852.1 18.4 copy-start.4
  1852.1 18.4 copy-start.5
  1862.9 7.7 copy-start
  1862.9 7.7 copy-start.1
Sparse Core Ops, SparseCore 0:
  1877.6 106.9 all-reduce.6
where the time goes:
time: 2000 us; the launch traced here: 1990 us
  blocking collectives  1620 us (81%)
  matrix products  170 us (8%)
  waiting for transfers between devices  115 us (6%)
  starting transfers between devices  39.2 us (2%)
  local copies, waits for them, and re-layouts  32.9 us (2%)
    psum x6, blocking collectives, shards(): lax.psum((local_dot(dir_bar, direction), local_dot(target, direction)), '...  745 us
    psum x4, blocking collectives, norm_sum(): return lax.psum(local_dot(first_vec, second_vec), 'sub')  507 us
    psum x3, blocking collectives, shards(): curvature = lax.psum(local_dot(direction, applied), 'sub')  366 us
    psum x1, waiting for transfers between devices, shards(): grad_sum = lax.psum(grad_sum, 'rhs')  106 us
    dot_general x8, matrix products, block_product(): return jnp.einsum('nkab,rnkb->rna', blocks, gathered, precision=highest)  84.9 us
  transfers between devices with their start and end apart: 17, of which 5 were waited for; matrix products, arithmetic and copies ran while one was open for 1% of the time, Pallas kernels for 0%

commit v1 on v0

--- a/solution.py
+++ b/solution.py
@@ -9,6 +9,12 @@
 IF = 6
 ITERS = 4
 highest = lax.Precision.HIGHEST
+
+
+def summed_here(x, axis):
+    terms = lax.all_gather(x, axis, axis=0, tiled=False)
+    total = terms.sum(axis=0)
+    return total
 
 
 def with_halo(array, sides, width):
@@ -49,7 +55,7 @@
 
 
 def norm_sum(first_vec, second_vec):
-    return lax.psum(local_dot(first_vec, second_vec), "sub")
+    return summed_here(local_dot(first_vec, second_vec), "sub")
 
 
 def grad_term(projected, zeta_bar, weight_zeta, resid_vec):

time: 2000 us -> 2010 us (level)
    psum x4 -> x0, blocking collectives: 507 us -> none  [norm_sum(): return lax.psum(local_dot(first_vec, second_vec), 'sub')]
    unnamed x0 -> x4, blocking collectives: none -> 507 us
where the time goes in v1:
time: 2010 us; the launch traced here: 2000 us
  blocking collectives  1620 us (81%)
  matrix products  170 us (8%)
  waiting for transfers between devices  115 us (6%)
  starting transfers between devices  39.2 us (2%)
  local copies, waits for them, and re-layouts  36.5 us (2%)
    psum x6, blocking collectives, shards(): lax.psum((local_dot(dir_bar, direction), local_dot(target, direction)), '...  745 us
    unnamed x4, blocking collectives  507 us
    psum x3, blocking collectives, shards(): curvature = lax.psum(local_dot(direction, applied), 'sub')  366 us
    psum x1, waiting for transfers between devices, shards(): grad_sum = lax.psum(grad_sum, 'rhs')  106 us
    dot_general x8, matrix products, block_product(): return jnp.einsum('nkab,rnkb->rna', blocks, gathered, precision=highest)  84.9 us
  transfers between devices with their start and end apart: 17, of which 5 were waited for; matrix products, arithmetic and copies ran while one was open for 1% of the time, Pallas kernels for 0%

profile of v1, /device:TPU:1, one launch (start us, length us, event | category | flops | bytes accessed | tf_op | source)
XLA Modules:
  0.0 1998.8 jit_solution(3692403261892643792)
XLA Ops:
  10.1 2.2 reshape.65
  12.3 3.8 convolution_bitcast_fusion.22
  16.1 2.1 fusion.14
  18.9 4.6 collective-permute-start
  23.5 1.9 collective-permute-start.1
  25.8 10.6 reshape.66
  38.6 10.5 multiply_reduce_fusion.16
  49.4 127.8 %all-reduce.8 = (f32[128]{0:T(128)S(1)}, f32[2]{0:T(128)S(1)}) all-reduce(f32[128]{0:T(128)S(1)} %dynamic-update-slice, f32[2]{0:T(128)S(1)} %get-tuple-element.9), channel_id=2, replica_groups=mesh['sub'=64,'rhs'=4] {'sub'}, use_global_device_ids=true, to_apply=%add | all-reduce | flops 130 | bytes 1040
  177.4 3.8 convolution_bitcast_fusion.20
  181.2 2.2 multiply_reduce_fusion.15
  183.7 127.3 %all-reduce.1 = f32[128]{0:T(128)S(1)} all-reduce(f32[128]{0:T(128)S(1)} %dynamic-update-slice.1), channel_id=3, replica_groups=mesh['sub'=64,'rhs'=4] {'sub'}, use_global_device_ids=true, to_apply=%add.1 | all-reduce | flops 128 | bytes 1024
  312.0 1.9 collective-permute-start.2
  313.9 2.4 collective-permute-start.3
  316.3 2.5 collective-permute-done.3
  319.8 10.5 multiply_reduce_fusion.14
  330.3 122.2 %psum.106 = f32[2]{0:T(128)S(1)} all-reduce(f32[2]{0:T(128)S(1)} %get-tuple-element.46), channel_id=1, replica_groups=mesh['sub'=64,'rhs'=4] {'sub'}, use_global_device_ids=true, to_apply=%region_7.10 | all-reduce | flops 2 | bytes 16 | tf_op jit(solution)/shard_map/psum | solution.py:85
  452.6 3.8 convolution_bitcast_fusion.18
  456.3 2.2 multiply_reduce_fusion.13
  458.8 125.9 %all-reduce.2 = f32[128]{0:T(128)S(1)} all-reduce(f32[128]{0:T(128)S(1)} %dynamic-update-slice.2), channel_id=4, replica_groups=mesh['sub'=64,'rhs'=4] {'sub'}, use_global_device_ids=true, to_apply=%add.2 | all-reduce | flops 128 | bytes 1024
  587.6 2.4 collective-permute-start.5
  590.0 2.5 collective-permute-done.5
  593.5 10.5 multiply_reduce_fusion.12
  604.0 122.2 %psum.107 = f32[2]{0:T(128)S(1)} all-reduce(f32[2]{0:T(128)S(1)} %get-tuple-element.50), channel_id=1, replica_groups=mesh['sub'=64,'rhs'=4] {'sub'}, use_global_device_ids=true, to_apply=%region_11.14 | all-reduce | flops 2 | bytes 16 | tf_op jit(solution)/shard_map/psum | solution.py:85
  726.8 3.8 convolution_bitcast_fusion.16
  730.6 2.2 multiply_reduce_fusion.11
  733.1 125.9 %all-reduce.3 = f32[128]{0:T(128)S(1)} all-reduce(f32[128]{0:T(128)S(1)} %dynamic-update-slice.3), channel_id=5, replica_groups=mesh['sub'=64,'rhs'=4] {'sub'}, use_global_device_ids=true, to_apply=%add.3 | all-reduce | flops 128 | bytes 1024
  861.9 2.4 collective-permute-start.7
  864.4 2.4 collective-permute-done.7
  867.8 11.1 multiply_reduce_fusion.1
  878.9 122.0 %all-reduce.7 = (f32[2]{0:T(128)S(1)}, f32[2]{0:T(128)S(1)}) all-reduce(f32[2]{0:T(128)S(1)} %get-tuple-element.6, f32[2]{0:T(128)S(1)} %get-tuple-element.5), channel_id=1, replica_groups=mesh['sub'=64,'rhs'=4] {'sub'}, use_global_device_ids=true, to_apply=%region_15.18 | all-reduce | flops 4 | bytes 32 | tf_op jit(solution)/shard_map/psum | solution.py:85
  1002.2 1.9 collective-permute-start.8
  1004.1 4.2 collective-permute-start.9
  1010.0 10.5 multiply_reduce_fusion.8
  1020.5 123.4 %psum.110 = f32[2]{0:T(128)S(1)} all-reduce(f32[2]{0:T(128)S(1)} %get-tuple-element.55), channel_id=1, replica_groups=mesh['sub'=64,'rhs'=4] {'sub'}, use_global_device_ids=true, to_apply=%region_19.22 | all-reduce | flops 2 | bytes 16 | tf_op jit(solution)/shard_map/psum | solution.py:106
  1144.5 3.8 convolution_bitcast_fusion.14
  1148.3 2.2 multiply_reduce_fusion.6
  1150.5 5.2 fusion.64
  1155.8 124.5 %all-reduce.6 = (f32[2]{0:T(128)S(1)}, f32[2]{0:T(128)S(1)}) all-reduce(f32[2]{0:T(128)S(1)} %copy-done.42, f32[2]{0:T(128)S(1)} %get-tuple-element.57), channel_id=1, replica_groups=mesh['sub'=64,'rhs'=4] {'sub'}, use_global_device_ids=true, to_apply=%region_21.24 | all-reduce | flops 4 | bytes 32 | tf_op jit(solution)/shard_map/psum | solution.py:106
  1281.6 1.9 collective-permute-start.10
  1283.5 2.6 collective-permute-start.11
  1286.1 5.4 fusion.63
  1292.4 10.5 multiply_reduce_fusion.5
  1303.0 123.0 %psum.113 = f32[2]{0:T(128)S(1)} all-reduce(f32[2]{0:T(128)S(1)} %get-tuple-element.59), channel_id=1, replica_groups=mesh['sub'=64,'rhs'=4] {'sub'}, use_global_device_ids=true, to_apply=%region_25.28 | all-reduce | flops 2 | bytes 16 | tf_op jit(solution)/shard_map/psum | solution.py:106
  1426.6 3.8 convolution_bitcast_fusion.12
  1430.4 2.2 multiply_reduce_fusion.3
  1432.6 5.2 fusion.66
  1437.8 125.2 %all-reduce.5 = (f32[2]{0:T(128)S(1)}, f32[2]{0:T(128)S(1)}) all-reduce(f32[2]{0:T(128)S(1)} %copy-done.41, f32[2]{0:T(128)S(1)} %get-tuple-element.61), channel_id=1, replica_groups=mesh['sub'=64,'rhs'=4] {'sub'}, use_global_device_ids=true, to_apply=%region_27.30 | all-reduce | flops 4 | bytes 32 | tf_op jit(solution)/shard_map/psum | solution.py:106
  1565.7 2.7 collective-permute-start.13
  1568.4 5.3 fusion.65
  1574.6 10.5 multiply_reduce_fusion.2
  1585.1 123.3 %psum.116 = f32[2]{0:T(128)S(1)} all-reduce(f32[2]{0:T(128)S(1)} %get-tuple-element.63), channel_id=1, replica_groups=mesh['sub'=64,'rhs'=4] {'sub'}, use_global_device_ids=true, to_apply=%region_31.34 | all-reduce | flops 2 | bytes 16 | tf_op jit(solution)/shard_map/psum | solution.py:106
  1708.5 3.8 convolution_bitcast_fusion.10
  1712.2 2.2 multiply_reduce_fusion
  1714.5 5.2 fusion.68
  1719.7 125.2 %all-reduce.4 = (f32[2]{0:T(128)S(1)}, f32[2]{0:T(128)S(1)}) all-reduce(f32[2]{0:T(128)S(1)} %copy-done.40, f32[2]{0:T(128)S(1)} %get-tuple-element.65), channel_id=1, replica_groups=mesh['sub'=64,'rhs'=4] {'sub'}, use_global_device_ids=true, to_apply=%region_33.36 | all-reduce | flops 4 | bytes 32 | tf_op jit(solution)/shard_map/psum | solution.py:106
  1847.6 2.6 collective-permute-start.15
  1850.2 5.3 fusion.67
  1856.5 10.8 fusion.1
  1867.3 3.8 convolution_bitcast_fusion.8
  1871.0 3.9 fusion.69
  1874.9 4.3 add_add_fusion
  1879.3 2.5 reshape.69
  1882.6 106.4 %all-reduce.11.cloned.1.call-done = f32[48,9216]{1,0:T(8,128)} async-done(((f32[48,9216]{1,0:T(8,128)}), f32[48,9216]{1,0:T(8,128)}) %all-reduce.11.cloned.1.call-update) | async-done | bytes 1769488 | tf_op jit(solution)/shard_map/psum | solution.py:131
  1988.9 2.8 copy.80
  (209 shorter events, 30.5 us)
Async XLA Ops:
  7.2 1981.8 %all-reduce.11.cloned.1.call-start = ((), (), s32[]{:S(2)}) async-start(), calls=%async_computation | async-start | bytes 3538944 | tf_op jit(solution)/shard_map/psum | solution.py:131
  12.3 13.1 copy-start.13
  18.9 18.7 collective-permute-start
  23.5 14.1 collective-permute-start.1
  25.8 10.6 copy-start.45
  177.1 6.3 copy-start.43
  177.3 133.9 %copy-start.14 = (f32[2]{0:T(128)}, f32[2]{0:T(128)S(1)}, u32[]{:S(2)}) copy-start(f32[2]{0:T(128)S(1)} %reduce_sum.199) | copy-start | bytes 28
  181.2 149.1 %copy-start.6 = (f32[2,48,96]{2,0,1:T(2,128)}, f32[2,48,96]{2,0,1:T(2,128)S(1)}, u32[]{:S(2)}) copy-start(f32[2,48,96]{2,0,1:T(2,128)S(1)} %convolution_bitcast_fusion.20) | copy-start | bytes 110596
  311.2 0.7 copy-start.18
  312.0 4.3 collective-permute-start.2
  313.9 4.9 collective-permute-start.3
  452.5 6.1 copy-start.23
  456.3 128.6 %copy-start.8 = (f32[2,48,96]{2,0,1:T(2,128)}, f32[2,48,96]{2,0,1:T(2,128)S(1)}, u32[]{:S(2)}) copy-start(f32[2,48,96]{2,0,1:T(2,128)S(1)} %convolution_bitcast_fusion.18) | copy-start | bytes 110596
  584.9 19.0 copy-start.20
  585.7 4.3 collective-permute-start.4
  587.6 4.9 collective-permute-start.5
  726.2 0.5 copy-start.25
  726.8 137.5 %copy-start.12 = (f32[2,4608]{1,0:T(2,128)S(1)}, f32[2,4608]{1,0:T(2,128)}, u32[]{:S(2)}) copy-start(f32[2,4608]{1,0:T(2,128)} %param.14) | copy-start | bytes 110596
  730.6 131.3 %copy-start.10 = (f32[2,48,96]{2,0,1:T(2,128)}, f32[2,48,96]{2,0,1:T(2,128)S(1)}, u32[]{:S(2)}) copy-start(f32[2,48,96]{2,0,1:T(2,128)S(1)} %convolution_bitcast_fusion.16) | copy-start | bytes 110596
  859.2 141.7 %copy-start.16 = (f32[2]{0:T(128)}, f32[2]{0:T(128)S(1)}, u32[]{:S(2)}) copy-start(f32[2]{0:T(128)S(1)} %reduce_sum.208) | copy-start | bytes 28
  859.2 0.7 copy-start.22
  860.0 4.5 collective-permute-start.6
  861.9 4.9 collective-permute-start.7
  1000.9 0.6 copy-start.36
  1000.9 0.6 copy-start.38
  1002.2 6.2 collective-permute-start.8
  1004.1 4.9 collective-permute-start.9
  1010.0 134.0 %copy-start.37 = (f32[2]{0:T(128)S(1)}, f32[2]{0:T(128)}, u32[]{:S(2)}) copy-start(f32[2]{0:T(128)} %copy-done.36) | copy-start | bytes 28
  1010.0 133.9 %copy-start.39 = (f32[2]{0:T(128)S(1)}, f32[2]{0:T(128)}, u32[]{:S(2)}) copy-start(f32[2]{0:T(128)} %copy-done.38) | copy-start | bytes 28
  1144.0 0.6 copy-start.30
  1148.3 7.5 copy-start.42
  1148.3 132.0 %copy-start.26 = (f32[2]{0:T(128)S(1)}, f32[2]{0:T(128)}, u32[]{:S(2)}) copy-start(f32[2]{0:T(128)} %copy-done.25) | copy-start | bytes 28
  1148.3 137.8 %copy-start.11 = (f32[2,48,96]{2,0,1:T(2,128)S(1)}, f32[2,48,96]{2,0,1:T(2,128)}, u32[]{:S(2)}) copy-start(f32[2,48,96]{2,0,1:T(2,128)} %copy-done.10) | copy-start | bytes 110596
  1280.3 0.5 copy-start.32
  1280.3 0.6 copy-start.34
  1281.6 9.9 collective-permute-start.10
  1283.5 8.0 collective-permute-start.11
  1292.4 133.6 %copy-start.17 = (f32[2]{0:T(128)S(1)}, f32[2]{0:T(128)}, u32[]{:S(2)}) copy-start(f32[2]{0:T(128)} %copy-done.16) | copy-start | bytes 28
  1292.4 133.6 %copy-start.27 = (f32[2]{0:T(128)S(1)}, f32[2]{0:T(128)}, u32[]{:S(2)}) copy-start(f32[2]{0:T(128)} %copy-done.25) | copy-start | bytes 28
  1292.4 133.5 %copy-start.31 = (f32[2]{0:T(128)S(1)}, f32[2]{0:T(128)}, u32[]{:S(2)}) copy-start(f32[2]{0:T(128)} %copy-done.30) | copy-start | bytes 28
  1292.4 133.5 %copy-start.33 = (f32[2]{0:T(128)S(1)}, f32[2]{0:T(128)}, u32[]{:S(2)}) copy-start(f32[2]{0:T(128)} %copy-done.32) | copy-start | bytes 28
  1292.4 133.5 %copy-start.35 = (f32[2]{0:T(128)S(1)}, f32[2]{0:T(128)}, u32[]{:S(2)}) copy-start(f32[2]{0:T(128)} %copy-done.34) | copy-start | bytes 28
  1426.0 0.5 copy-start.28
  1430.4 7.5 copy-start.41
  1430.4 132.6 %copy-start.24 = (f32[2]{0:T(128)S(1)}, f32[2]{0:T(128)}, u32[]{:S(2)}) copy-start(f32[2]{0:T(128)} %copy-done.23) | copy-start | bytes 28
  1430.4 138.0 %copy-start.9 = (f32[2,48,96]{2,0,1:T(2,128)S(1)}, f32[2,48,96]{2,0,1:T(2,128)}, u32[]{:S(2)}) copy-start(f32[2,48,96]{2,0,1:T(2,128)} %copy-done.8) | copy-start | bytes 110596
  1432.6 142.0 %copy-start.21 = (f32[2]{0:T(128)S(1)}, f32[2]{0:T(128)}, u32[]{:S(2)}) copy-start(f32[2]{0:T(128)} %copy-done.20) | copy-start | bytes 28
  1563.8 9.9 collective-permute-start.12
  1565.7 8.0 collective-permute-start.13
  1574.6 133.8 %copy-start.15 = (f32[2]{0:T(128)S(1)}, f32[2]{0:T(128)}, u32[]{:S(2)}) copy-start(f32[2]{0:T(128)} %copy-done.14) | copy-start | bytes 28
  1574.6 133.8 %copy-start.29 = (f32[2]{0:T(128)S(1)}, f32[2]{0:T(128)}, u32[]{:S(2)}) copy-start(f32[2]{0:T(128)} %copy-done.28) | copy-start | bytes 28
  1712.2 7.5 copy-start.40
  1712.2 132.6 %copy-start.44 = (f32[2]{0:T(128)S(1)}, f32[2]{0:T(128)}, u32[]{:S(2)}) copy-start(f32[2]{0:T(128)} %copy-done.43) | copy-start | bytes 28
  1712.2 138.0 %copy-start.7 = (f32[2,48,96]{2,0,1:T(2,128)S(1)}, f32[2,48,96]{2,0,1:T(2,128)}, u32[]{:S(2)}) copy-start(f32[2,48,96]{2,0,1:T(2,128)} %copy-done.6) | copy-start | bytes 110596
  1714.5 142.0 %copy-start.19 = (f32[2]{0:T(128)S(1)}, f32[2]{0:T(128)}, u32[]{:S(2)}) copy-start(f32[2]{0:T(128)} %copy-done.18) | copy-start | bytes 28
  1845.7 9.8 collective-permute-start.14
  1847.6 7.9 collective-permute-start.15
  1856.4 18.4 copy-start.2
  1856.5 18.4 copy-start.3
  1856.5 18.4 copy-start.4
  1856.5 18.4 copy-start.5
  1867.3 7.7 copy-start
  1867.3 7.7 copy-start.1
Sparse Core Ops, SparseCore 0:
  1882.0 106.9 all-reduce.10
